TPU v7x, 32 devices: a whole 2x2x4 slice. The times are simulated.
32 devices in a mesh: dp: 8 (over z, x), tensor: 4 (over y, core).
Axes of the slice: x: 2, y: 2, z: 4, core: 2. Of those that a mesh axis runs over, the one named last changes fastest.
Arguments:
- inputs: bfloat16 [8192, 4096], P('dp'), may hold values from -6 to 6
- out_grads: bfloat16 [8192, 6144], P('dp', 'tensor'), may hold values from -0.01953125 to 0.01953125
- left_factor: float32 [4096, 4096], P('dp', 'tensor'), may hold values from -6 to 6
- right_factor: float32 [6144, 6144], P('dp', 'tensor'), may hold values from -6 to 6
- left_basis: float32 [4096, 4096], P('dp', 'tensor'), may hold values from -0.09375 to 0.09375
- right_basis: float32 [6144, 6144], P('dp', 'tensor'), may hold values from -0.078125 to 0.078125
Outputs:
- left_new: float32 [4096, 4096], P('dp', 'tensor')
- right_new: float32 [6144, 6144], P('dp', 'tensor')
- rotated: float32 [4096, 6144], P('dp', 'tensor')
All inputs are finite; a program needn't handle non-finite values.
Results may differ from a plain program's by a relative error of at most 0.019.
Values may be sent and summed in bfloat16 or wider, within the bound.
A program may use at most 192 MiB of HBM per device.

v0:
```python
import jax
import jax.numpy as jnp
from jax import lax
from jax.sharding import PartitionSpec as P


def shards(inputs, out_grads, left_factor, right_factor, left_basis, right_basis):
    krows = left_factor.shape[0]
    mrows = right_factor.shape[0]
    mcols = out_grads.shape[1]
    right_low = right_basis.astype(jnp.bfloat16)
    left_low = left_basis.astype(jnp.bfloat16)
    summed = lax.psum_scatter(
        lax.dot_general(
            inputs, out_grads, (((0,), (0,)), ((), ())), preferred_element_type=jnp.float32
        ).astype(jnp.bfloat16),
        "dp",
        scatter_dimension=0,
        tiled=True,
    )
    col_panel, basis_panel = (
        lax.all_gather(summed, "dp", axis=0, tiled=True),
        lax.all_gather(right_low, "dp", axis=0, tiled=True),
    )
    row_panel, left_rows = (
        lax.all_gather(summed, "tensor", axis=1, tiled=True),
        lax.all_gather(left_low, "tensor", axis=1, tiled=True),
    )
    gram_left = lax.psum_scatter(
        lax.dot_general(
            col_panel, summed, (((1,), (1,)), ((), ())), preferred_element_type=jnp.float32
        ).astype(jnp.bfloat16),
        "tensor",
        scatter_dimension=0,
        tiled=True,
    ).astype(jnp.float32)
    left_new = 0.95 * left_factor + 0.05 * gram_left.T
    turned = jnp.dot(row_panel, basis_panel, preferred_element_type=jnp.float32).astype(
        jnp.bfloat16
    )
    stride = mrows + krows
    blocks = lax.axis_size("dp") * stride // stride
    right_part = lax.dot_general(
        row_panel, summed, (((0,), (0,)), ((), ())), preferred_element_type=jnp.float32
    )
    rot_part = lax.dot_general(
        left_rows, turned, (((0,), (0,)), ((), ())), preferred_element_type=jnp.float32
    )
    joined = jnp.concatenate(
        [right_part.reshape(blocks, mrows, mcols), rot_part.reshape(blocks, krows, mcols)], axis=1
    )
    together = lax.psum_scatter(
        joined.reshape(blocks * stride, mcols).astype(jnp.bfloat16),
        "dp",
        scatter_dimension=0,
        tiled=True,
    ).astype(jnp.float32)
    right_new = 0.95 * right_factor + 0.05 * together[:mrows]
    rotated = together[mrows:]
    return (left_new, right_new, rotated)


def solution(mesh):
    return jax.shard_map(
        shards,
        mesh=mesh,
        in_specs=(
            P("dp", None),
            P("dp", "tensor"),
            P("dp", "tensor"),
            P("dp", "tensor"),
            P("dp", "tensor"),
            P("dp", "tensor"),
        ),
        out_specs=(P("dp", "tensor"), P("dp", "tensor"), P("dp", "tensor")),
        check_vma=False,
    )
```

profile of v0, /device:TPU:0, one launch (start us, length us, event | category | flops | bytes accessed | tf_op | source)
XLA Modules:
  0.0 1462.3 jit_solution(1834453289369584762)
XLA Ops:
  7.2 0.0 copy-start
  7.2 0.0 reduce-scatter.4.cloned.1.call-start
  7.2 1.8 copy-done
  9.1 19.2 %convolution_convert_fusion.2 = bf16[4096,1536]{1,0:T(8,128)(2,1)} fusion(bf16[1024,4096]{1,0:T(8,128)(2,1)} %param.6, bf16[1024,1536]{1,0:T(8,128)(2,1)S(1)} %copy-done), kind=kOutput, calls=%fused_computation.3 | convolution fusion | flops 12891193344 | bytes 24117248 | tf_op jit(solution)/shard_map/dot_general | solution.py:14
  28.2 0.0 copy-start.4
  28.2 0.0 reduce-scatter.4.cloned.1.call-update
  28.3 0.0 all-gather.5.cloned.1.call-start
  28.3 210.1 %reduce-scatter.4.cloned.1.call-done = bf16[512,1536]{1,0:T(8,128)(2,1)} async-done(((bf16[4096,1536]{1,0:T(8,128)(2,1)}), bf16[512,1536]{1,0:T(8,128)(2,1)}) %reduce-scatter.4.cloned.1.call-update) | async-done | bytes 1572880 | tf_op jit(solution)/shard_map/reduce_scatter | solution.py:13
  238.4 0.0 all-gather.5.cloned.1.call-update
  238.4 0.0 all-gather.11.cloned.1.call-start
  238.5 0.0 copy-done.4
  238.5 1.1 convert_element_type.30
  239.6 0.0 all-gather.11.cloned.1.call-update
  239.6 0.0 copy-start.3
  239.6 0.0 all-gather.9.cloned.1.call-start
  239.7 4.1 convert_element_type.28
  243.8 0.0 all-gather.9.cloned.1.call-update
  243.8 0.0 all-gather.7.cloned.1.call-start
  243.9 0.5 all-gather.7.cloned.1.call-update
  244.4 0.0 reduce-scatter.6.cloned.1.call-start
  244.5 171.6 %all-gather.5.cloned.1.call-done = bf16[4096,1536]{1,0:T(8,128)(2,1)} async-done(((bf16[512,1536]{1,0:T(8,128)(2,1)}), bf16[4096,1536]{1,0:T(8,128)(2,1)}) %all-gather.5.cloned.1.call-update) | async-done | bytes 12582928 | tf_op jit(solution)/shard_map/all_gather | solution.py:22
  416.1 0.0 copy-done.3
  416.1 12.9 convolution_convert_fusion.3
  429.0 0.0 reduce-scatter.6.cloned.1.call-update
  429.0 0.2 reduce-scatter.8.cloned.1.call-start
  429.2 21.7 %all-gather.11.cloned.1.call-done = bf16[512,4096]{1,0:T(8,128)(2,1)} async-done(((bf16[512,1024]{1,0:T(8,128)(2,1)}), bf16[512,4096]{1,0:T(8,128)(2,1)}) %all-gather.11.cloned.1.call-update) | async-done | bytes 4194320 | tf_op jit(solution)/shard_map/all_gather | solution.py:27
  451.0 364.5 %all-gather.9.cloned.1.call-done = bf16[6144,1536]{1,0:T(8,128)(2,1)} async-done(((bf16[768,1536]{1,0:T(8,128)(2,1)}), bf16[6144,1536]{1,0:T(8,128)(2,1)}) %all-gather.9.cloned.1.call-update) | async-done | bytes 18874384 | tf_op jit(solution)/shard_map/all_gather | solution.py:23
  815.4 47.8 %all-gather.7.cloned.1.call-done = bf16[512,6144]{1,0:T(8,128)(2,1)} async-done(((bf16[512,1536]{1,0:T(8,128)(2,1)}), bf16[512,6144]{1,0:T(8,128)(2,1)}) %all-gather.7.cloned.1.call-update) | async-done | bytes 6291472 | tf_op jit(solution)/shard_map/all_gather | solution.py:26
  863.2 32.4 %fusion = bf16[4096,1536]{0,1:T(8,128)(2,1)} fusion(bf16[512,4096]{1,0:T(8,128)(2,1)} %all-gather.11.cloned.1.call-done, bf16[512,6144]{1,0:T(8,128)(2,1)} %all-gather.7.cloned.1.call-done, bf16[6144,1536]{1,0:T(8,128)(2,1)} %all-gather.9.cloned.1.call-done), kind=kOutput, calls=%fused_computation.4 | convolution fusion | flops 16113205248 | bytes 41943040 | tf_op jit(solution)/shard_map/dot_general | solution.py:46
  895.6 16.6 %copy.12 = bf16[4096,1536]{1,0:T(8,128)(2,1)} copy(bf16[4096,1536]{0,1:T(8,128)(2,1)} %fusion) | data formatting | bytes 25165824 | tf_op jit(solution)/shard_map/reshape | solution.py:50
  912.2 15.9 %convolution_convert_fusion = bf16[6144,1536]{1,0:T(8,128)(2,1)} fusion(bf16[512,6144]{1,0:T(8,128)(2,1)} %all-gather.7.cloned.1.call-done, bf16[512,1536]{1,0:T(8,128)(2,1)S(1)} %copy-done.3), kind=kOutput, calls=%fused_computation.1 | convolution fusion | flops 9673113600 | bytes 26738688 | tf_op jit(solution)/shard_map/dot_general | solution.py:43
  928.1 21.8 %pad_maximum_fusion = bf16[8,1280,1536]{2,1,0:T(8,128)(2,1)} fusion(bf16[8,512,1536]{2,1,0:T(8,128)(2,1)} %bitcast.17, bf16[8,768,1536]{2,1,0:T(8,128)(2,1)} %bitcast.18), kind=kLoop, calls=%fused_computation | loop fusion | flops 62914560 | bytes 62914560 | tf_op jit(solution)/shard_map/concatenate | solution.py:49
  950.0 0.0 reduce-scatter.8.cloned.1.call-update
  950.0 1.9 copy.9
  951.9 0.0 reduce-scatter.6.cloned.1.call-done
  951.9 2.9 bitcast_add_fusion
  954.8 3.0 copy.11
  957.8 486.5 %reduce-scatter.8.cloned.1.call-done = bf16[1280,1536]{1,0:T(8,128)(2,1)} async-done(((bf16[10240,1536]{1,0:T(8,128)(2,1)}), bf16[1280,1536]{1,0:T(8,128)(2,1)}) %reduce-scatter.8.cloned.1.call-update) | async-done | bytes 3932176 | tf_op jit(solution)/shard_map/reduce_scatter | solution.py:52
  1444.3 3.2 convert_element_type.32
  1447.5 0.0 copy-start.2
  1447.5 0.0 copy-start.1
  1447.5 5.8 fusion.1
  1453.3 0.0 copy-done.2
  1453.3 2.1 slice.9
  1455.4 0.0 copy-done.1
Async XLA Ops:
  7.2 1.9 copy-start
  7.2 231.2 %reduce-scatter.4.cloned.1.call-start = ((), (), s32[]{:S(2)}) async-start(), calls=%async_computation.3 | async-start | bytes 14155776 | tf_op jit(solution)/shard_map/reduce_scatter | solution.py:13
  28.2 210.2 %copy-start.4 = (f32[512,1024]{1,0:T(8,128)S(1)}, f32[512,1024]{1,0:T(8,128)}, u32[]{:S(2)}) copy-start(f32[512,1024]{1,0:T(8,128)} %param.10) | copy-start | bytes 6291460
  28.3 387.9 %all-gather.5.cloned.1.call-start = ((), (), s32[]{:S(2)}) async-start(), calls=%async_computation.4 | async-start | bytes 14155776 | tf_op jit(solution)/shard_map/all_gather | solution.py:22
  238.4 212.6 %all-gather.11.cloned.1.call-start = ((), (), s32[]{:S(2)}) async-start(), calls=%async_computation.8 | async-start | bytes 5242880 | tf_op jit(solution)/shard_map/all_gather | solution.py:27
  239.6 176.5 %copy-start.3 = (bf16[512,1536]{1,0:T(8,128)(2,1)S(1)}, bf16[512,1536]{1,0:T(8,128)(2,1)}, u32[]{:S(2)}) copy-start(bf16[512,1536]{1,0:T(8,128)(2,1)} %reduce-scatter.4.cloned.1.call-done) | copy-start | bytes 4718596
  239.6 575.8 %all-gather.9.cloned.1.call-start = ((), (), s32[]{:S(2)}) async-start(), calls=%async_computation.7 | async-start | bytes 21233664 | tf_op jit(solution)/shard_map/all_gather | solution.py:23
  243.8 619.4 %all-gather.7.cloned.1.call-start = ((), (), s32[]{:S(2)}) async-start(), calls=%async_computation.6 | async-start | bytes 7864320 | tf_op jit(solution)/shard_map/all_gather | solution.py:26
  244.4 707.5 %reduce-scatter.6.cloned.1.call-start = ((), (), s32[]{:S(2)}) async-start(), calls=%async_computation.5 | async-start | bytes 5242880 | tf_op jit(solution)/shard_map/reduce_scatter | solution.py:29
  429.0 1015.3 %reduce-scatter.8.cloned.1.call-start = ((), (), s32[]{:S(2)}) async-start(), calls=%async_computation.9 | async-start | bytes 35389440 | tf_op jit(solution)/shard_map/reduce_scatter | solution.py:52
  1447.5 5.8 copy-start.2
  1447.5 7.9 copy-start.1
Sparse Core Ops, SparseCore 0:
  28.4 209.9 reduce-scatter.3
  240.6 175.4 all-gather.4
  418.3 32.6 all-gather.10
  452.9 362.4 all-gather.8
  816.8 46.3 all-gather.6
  866.2 44.4 reduce-scatter.5
  950.1 494.1 reduce-scatter.7
where the time goes:
time: 1460 us
  waiting for transfers between devices  1300 us (89%)
  matrix products  80.3 us (6%)
  other arithmetic  39 us (3%)
  local copies, waits for them, and re-layouts  25.4 us (2%)
    reduce_scatter x1, waiting for transfers between devices, shards(): lax.psum_scatter(joined.reshape(blocks * stride, mcols).astype(jnp.bfloat...  486 us
    all_gather x1, waiting for transfers between devices, shards(): lax.all_gather(right_low, 'dp', axis=0, tiled=True)  364 us
    reduce_scatter x1, waiting for transfers between devices, shards(): lax.psum_scatter(lax.dot_general(inputs, out_grads, (((0,), (0,)), ((), (...  210 us
    all_gather x1, waiting for transfers between devices, shards(): lax.all_gather(summed, 'dp', axis=0, tiled=True)  172 us
    all_gather x1, waiting for transfers between devices, shards(): lax.all_gather(summed, 'tensor', axis=1, tiled=True)  47.8 us
    dot_general x1, matrix products, shards(): lax.dot_general(left_rows, turned, (((0,), (0,)), ((), ())), preferred_el...  32.4 us
  transfers between devices with their start and end apart: 7, of which 6 were waited for; matrix products, arithmetic and copies ran while one was open for 8% of the time, Pallas kernels for 0%

commit v1 on v0

v1 whole, which is shorter than its diff:
```python
import jax
import jax.numpy as jnp
from jax import lax
from jax.sharding import PartitionSpec as P

F32 = jnp.float32
BF16 = jnp.bfloat16


def mm(a, b, ca, cb):
    return lax.dot_general(a, b, (((ca,), (cb,)), ((), ())), preferred_element_type=F32)


def spread(block, owner, n_dp, n_t):
    me = lax.axis_index("tensor")
    mine = lax.rem(me - owner(lax.axis_index("dp")) + n_t, n_t)
    step = 1
    while step < n_t:
        pairs = []
        for d in range(n_dp):
            for k in range(step):
                if k + step < n_t:
                    src = (owner(d) + k) % n_t
                    dst = (owner(d) + k + step) % n_t
                    pairs.append((d * n_t + src, d * n_t + dst))
        got = lax.ppermute(block, ("dp", "tensor"), pairs)
        block = jnp.where((mine >= step) & (mine < 2 * step), got, block)
        step *= 2
    return block


def shards(inputs, out_grads, left_factor, right_factor, left_basis, right_basis):
    n_dp, n_t = lax.axis_size("dp"), lax.axis_size("tensor")
    krows, kcols = left_factor.shape
    mrows, mcols = right_factor.shape
    dp = lax.axis_index("dp")
    left_low = left_basis.astype(BF16)
    left_rows = lax.all_gather(left_low, "tensor", axis=1, tiled=True)
    left_cols = lax.all_to_all(left_rows, "dp", split_axis=1, concat_axis=0, tiled=True)
    basis_panel = lax.all_gather(right_basis.astype(BF16), "dp", axis=0, tiled=True)
    summed = lax.psum_scatter(
        mm(inputs, out_grads, 0, 0).astype(BF16), "dp", scatter_dimension=0, tiled=True
    )
    col_panel = lax.all_gather(summed, "dp", axis=0, tiled=True)
    turned = mm(left_cols, col_panel, 0, 0).astype(BF16)
    turned_rows = lax.all_gather(turned, "tensor", axis=1, tiled=True)
    own = lax.dynamic_slice_in_dim(col_panel, lax.rem(dp * mrows, mcols), mrows, 1)
    own = spread(own, lambda d: d * mrows // mcols, n_dp, n_t)
    parts = jnp.einsum(
        "jkc,rc->jrk", col_panel.reshape(n_t, kcols, mcols), summed, preferred_element_type=F32
    ).astype(BF16)
    gram_left = lax.psum_scatter(
        parts.reshape(n_t * krows, kcols), "tensor", scatter_dimension=0, tiled=True
    ).astype(F32)
    left_new = 0.95 * left_factor + 0.05 * gram_left
    right_new = 0.95 * right_factor + 0.05 * mm(own, col_panel, 0, 0)
    rotated = mm(turned_rows, basis_panel, 1, 0)
    return left_new, right_new, rotated


def solution(mesh):
    spec = P("dp", "tensor")
    return jax.shard_map(
        shards,
        mesh=mesh,
        in_specs=(P("dp", None), spec, spec, spec, spec, spec),
        out_specs=(spec, spec, spec),
        check_vma=False,
    )
```

time: 1460 us -> 976 us (0.67)
  waiting for transfers between devices: 1300 us -> 831 us
  other arithmetic: 39 us -> 17.4 us
  starting transfers between devices: 0.46 us -> 15.3 us
    reduce_scatter x3 -> x2, waiting for transfers between devices: 697 us -> 210 us  [the longest x1 210 us: shards(): lax.psum_scatter(mm(inputs, out_grads, 0, 0).astype(BF16), 'dp', scatter_...]
    all_to_all x0 -> x1, waiting for transfers between devices: none -> 102 us  [shards(): lax.all_to_all(left_rows, 'dp', split_axis=1, concat_axis=0, tiled=True)]
    all_gather x4, waiting for transfers between devices: 606 us -> 519 us  [the longest x1 274 us: shards(): lax.all_gather(right_basis.astype(BF16), 'dp', axis=0, tiled=True)]
    concatenate x1 -> x0, other arithmetic: 21.8 us -> none  [shards(): jnp.concatenate([right_part.reshape(blocks, mrows, mcols), rot_part.resha...]
    reshape x1 -> x0, local copies, waits for them, and re-layouts: 16.6 us -> none  [shards(): rot_part.reshape(blocks, krows, mcols)]
    dot_general x4 -> x5, matrix products: 80.3 us -> 77.6 us  [the longest x4 66.1 us: mm(): lax.dot_general(a, b, (((ca,), (cb,)), ((), ())), preferred_element_type=...]
  transfers between devices with their start and end apart: 7 -> 9, of which waited for: 6 -> 6; matrix products, arithmetic and copies ran while one was open for 8% -> 8% of each run, Pallas kernels for 0% -> 0%
where the time goes in v1:
time: 976 us; the launch traced here: 975 us
  waiting for transfers between devices  831 us (85%)
  matrix products  77.6 us (8%)
  local copies, waits for them, and re-layouts  19.6 us (2%)
  other arithmetic  17.4 us (2%)
  starting transfers between devices  15.3 us (2%)
  between operations  14.2 us (1%)
    all_gather x1, waiting for transfers between devices, shards(): lax.all_gather(right_basis.astype(BF16), 'dp', axis=0, tiled=True)  274 us
    reduce_scatter x1, waiting for transfers between devices, shards(): lax.psum_scatter(mm(inputs, out_grads, 0, 0).astype(BF16), 'dp', scatter_...  210 us
    all_gather x1, waiting for transfers between devices, shards(): col_panel = lax.all_gather(summed, 'dp', axis=0, tiled=True)  176 us
    all_to_all x1, waiting for transfers between devices, shards(): lax.all_to_all(left_rows, 'dp', split_axis=1, concat_axis=0, tiled=True)  102 us
    dot_general x4, matrix products, mm(): lax.dot_general(a, b, (((ca,), (cb,)), ((), ())), preferred_element_type=...  66.1 us
    all_gather x1, waiting for transfers between devices, shards(): turned_rows = lax.all_gather(turned, 'tensor', axis=1, tiled=True)  49.6 us
  transfers between devices with their start and end apart: 9, of which 6 were waited for; matrix products, arithmetic and copies ran while one was open for 8% of the time, Pallas kernels for 0%

profile of v1, /device:TPU:0, one launch (start us, length us, event | category | flops | bytes accessed | tf_op | source)
XLA Modules:
  0.0 975.2 jit_solution(8591873962908227927)
XLA Ops:
  7.2 0.0 copy-start
  7.2 0.0 reduce-scatter.3.cloned.1.call-start
  7.2 1.8 copy-done
  9.1 19.1 %convolution_convert_fusion = bf16[4096,1536]{1,0:T(8,128)(2,1)} fusion(bf16[1024,4096]{1,0:T(8,128)(2,1)} %param.6, bf16[1024,1536]{1,0:T(8,128)(2,1)S(1)} %copy-done), kind=kOutput, calls=%fused_computation | convolution fusion | flops 12891193344 | bytes 24117248 | tf_op jit(solution)/shard_map/dot_general | solution.py:11
  28.2 0.0 copy-start.2
  28.2 0.0 reduce-scatter.3.cloned.1.call-update
  28.2 0.0 all-gather.5.cloned.1.call-start
  28.3 210.1 %reduce-scatter.3.cloned.1.call-done = bf16[512,1536]{1,0:T(8,128)(2,1)} async-done(((bf16[4096,1536]{1,0:T(8,128)(2,1)}), bf16[512,1536]{1,0:T(8,128)(2,1)}) %reduce-scatter.3.cloned.1.call-update) | async-done | bytes 1572880 | tf_op jit(solution)/shard_map/reduce_scatter | solution.py:41
  238.4 0.0 all-gather.5.cloned.1.call-update
  238.4 0.0 all-gather.7.cloned.1.call-start
  238.4 0.0 copy-done.2
  238.4 1.4 copy.9
  239.8 0.0 all-gather.7.cloned.1.call-update
  239.8 0.0 reduce-scatter.5.cloned.1.call-start
  239.9 176.2 %all-gather.5.cloned.1.call-done = bf16[4096,1536]{1,0:T(8,128)(2,1)} async-done(((bf16[512,1536]{1,0:T(8,128)(2,1)}), bf16[4096,1536]{1,0:T(8,128)(2,1)}) %all-gather.5.cloned.1.call-update) | async-done | bytes 12582928 | tf_op jit(solution)/shard_map/all_gather | solution.py:44
  416.1 11.4 %convolution_convert_fusion.2 = bf16[512,4,1024]{2,0,1:T(8,128)(2,1)} fusion(bf16[4,1024,1536]{2,1,0:T(8,128)(2,1)} %bitcast.20, bf16[512,1536]{1,0:T(8,128)(2,1)} %reduce-scatter.3.cloned.1.call-done), kind=kOutput, calls=%fused_computation.8 | convolution fusion | flops 6444548096 | bytes 18350080 | tf_op jit(solution)/shard_map/jkc,rc->jrk/dot_general | solution.py:49
  427.5 0.0 reduce-scatter.5.cloned.1.call-update
  427.6 0.0 all-gather.11.cloned.1.call-start
  427.6 4.0 convert_element_type.31
  431.6 0.0 all-gather.11.cloned.1.call-update
  431.7 19.3 %all-gather.7.cloned.1.call-done = bf16[512,4096]{0,1:T(8,128)(2,1)} async-done(((bf16[512,1024]{0,1:T(8,128)(2,1)}), bf16[512,4096]{0,1:T(8,128)(2,1)}) %all-gather.7.cloned.1.call-update) | async-done | bytes 4194320 | tf_op jit(solution)/shard_map/all_gather | solution.py:38
  450.9 5.5 all-to-all-start
  456.4 0.0 all-gather.9.cloned.1.call-start
  456.5 9.8 %constant_dynamic-slice_fusion = bf16[4096,768]{1,0:T(8,128)(2,1)} fusion(bf16[4096,1536]{1,0:T(8,128)(2,1)} %all-gather.5.cloned.1.call-done, s32[]{:T(128)S(6)} %select_n.25), kind=kLoop, calls=%fused_computation.11 | loop fusion | bytes 12582916 | tf_op jit(solution)/shard_map/dynamic_slice | solution.py:47
  466.3 4.3 collective-permute-start
  470.6 101.8 %all-to-all-done = bf16[512,8,512]{0,2,1:T(8,128)(2,1)} async-done(((bf16[512,8,512]{0,2,1:T(8,128)(2,1)}), bf16[512,8,512]{0,2,1:T(8,128)(2,1)}, u32[]{:S(2)}, u32[]{:S(2)}) %all-to-all-start) | async-done | bytes 4194336 | tf_op jit(solution)/shard_map/all_to_all | solution.py:39
  572.4 6.5 copy.10
  578.9 11.9 %fusion.5 = bf16[512,1536]{0,1:T(8,128)(2,1)} fusion(bf16[4096,1536]{1,0:T(8,128)(2,1)} %all-gather.5.cloned.1.call-done, bf16[4096,512]{1,0:T(8,128)(2,1)} %bitcast.23), kind=kOutput, calls=%fused_computation.7 | convolution fusion | flops 6443237376 | bytes 18350080 | tf_op jit(solution)/shard_map/dot_general | solution.py:11
  590.8 0.0 all-gather.9.cloned.1.call-update
  590.8 0.0 copy-start.3
  590.9 0.0 collective-permute-done
  590.9 10.3 %broadcast_select_fusion = bf16[4096,768]{1,0:T(8,128)(2,1)} fusion(bf16[4096,768]{1,0:T(8,128)(2,1)} %collective-permute-done, pred[]{:T(512)S(6)} %and.15, bf16[4096,1536]{1,0:T(8,128)(2,1)} %all-gather.5.cloned.1.call-done, s32[]{:T(128)S(6)} %select_n.25), kind=kLoop, calls=%fused_computation.3 | loop fusion | flops 3145728 | bytes 18874372 | tf_op jit(solution)/shard_map/jit(_where)/select_n | solution.py:27
  601.1 5.2 collective-permute-start.1
  606.4 0.0 reduce-scatter.5.cloned.1.call-done
  606.4 0.0 copy-done.3
  606.4 3.0 multiply_add_fusion.1
  609.4 274.1 %all-gather.11.cloned.1.call-done = bf16[6144,1536]{1,0:T(8,128)(2,1)} async-done(((bf16[768,1536]{1,0:T(8,128)(2,1)}), bf16[6144,1536]{1,0:T(8,128)(2,1)}) %all-gather.11.cloned.1.call-update) | async-done | bytes 18874384 | tf_op jit(solution)/shard_map/all_gather | solution.py:40
  883.6 49.6 %all-gather.9.cloned.1.call-done = bf16[512,6144]{0,1:T(8,128)(2,1)} async-done(((bf16[512,1536]{0,1:T(8,128)(2,1)}), bf16[512,6144]{0,1:T(8,128)(2,1)}) %all-gather.9.cloned.1.call-update) | async-done | bytes 6291472 | tf_op jit(solution)/shard_map/all_gather | solution.py:46
  933.2 16.9 %fusion.7 = f32[512,1536]{1,0:T(8,128)} fusion(bf16[512,6144]{0,1:T(8,128)(2,1)} %all-gather.9.cloned.1.call-done, bf16[6144,1536]{1,0:T(8,128)(2,1)} %all-gather.11.cloned.1.call-done), kind=kOutput, calls=%fused_computation.12 | convolution fusion | flops 9663676416 | bytes 28311552 | tf_op jit(solution)/shard_map/dot_general | solution.py:11
  950.1 0.0 collective-permute-done.1
  950.1 0.0 copy-start.1
  950.1 18.2 %multiply_add_fusion = f32[768,1536]{1,0:T(8,128)} fusion(f32[768,1536]{1,0:T(8,128)} %param.9, bf16[4096,1536]{1,0:T(8,128)(2,1)} %all-gather.5.cloned.1.call-done, bf16[4096,768]{1,0:T(8,128)(2,1)} %collective-permute-done.1, bf16[4096,768]{1,0:T(8,128)(2,1)} %broadcast_select_fusion, pred[]{:T(512)S(6)} %and.14), kind=kOutput, calls=%fused_computation.5 | convolution fusion | flops 9670361088 | bytes 34603008 | tf_op jit(solution)/shard_map/dot_general | solution.py:11
  968.3 0.0 copy-done.1
Async XLA Ops:
  7.2 1.9 copy-start
  7.2 231.2 %reduce-scatter.3.cloned.1.call-start = ((), (), s32[]{:S(2)}) async-start(), calls=%async_computation.3 | async-start | bytes 14155776 | tf_op jit(solution)/shard_map/reduce_scatter | solution.py:41
  28.2 210.2 %copy-start.2 = (f32[512,1024]{1,0:T(8,128)S(1)}, f32[512,1024]{1,0:T(8,128)}, u32[]{:S(2)}) copy-start(f32[512,1024]{1,0:T(8,128)} %param.10) | copy-start | bytes 6291460
  28.2 387.9 %all-gather.5.cloned.1.call-start = ((), (), s32[]{:S(2)}) async-start(), calls=%async_computation.4 | async-start | bytes 14155776 | tf_op jit(solution)/shard_map/all_gather | solution.py:44
  238.4 212.6 %all-gather.7.cloned.1.call-start = ((), (), s32[]{:S(2)}) async-start(), calls=%async_computation.6 | async-start | bytes 5242880 | tf_op jit(solution)/shard_map/all_gather | solution.py:38
  239.8 366.6 %reduce-scatter.5.cloned.1.call-start = ((), (), s32[]{:S(2)}) async-start(), calls=%async_computation.5 | async-start | bytes 5242880 | tf_op jit(solution)/shard_map/reduce_scatter | solution.py:52
  427.6 456.0 %all-gather.11.cloned.1.call-start = ((), (), s32[]{:S(2)}) async-start(), calls=%async_computation.8 | async-start | bytes 21233664 | tf_op jit(solution)/shard_map/all_gather | solution.py:40
  450.9 121.4 %all-to-all-start = ((bf16[512,8,512]{0,2,1:T(8,128)(2,1)}), bf16[512,8,512]{0,2,1:T(8,128)(2,1)}, u32[]{:S(2)}, u32[]{:S(2)}) async-start(bf16[512,8,512]{0,2,1:T(8,128)(2,1)} %bitcast.22), calls=%async_computation.2 | async-start | bytes 8388608 | tf_op jit(solution)/shard_map/all_to_all | solution.py:39
  456.4 476.8 %all-gather.9.cloned.1.call-start = ((), (), s32[]{:S(2)}) async-start(), calls=%async_computation.7 | async-start | bytes 7864320 | tf_op jit(solution)/shard_map/all_gather | solution.py:46
  466.3 124.5 %collective-permute-start = (bf16[4096,768]{1,0:T(8,128)(2,1)}, bf16[4096,768]{1,0:T(8,128)(2,1)}, u32[]{:S(2)}, u32[]{:S(2)}) collective-permute-start(bf16[4096,768]{1,0:T(8,128)(2,1)} %constant_dynamic-slice_fusion), channel_id=1, source_target_pairs={{0,1},{4,5},{9,10},{13,14},{18,19},{22,23},{27,24},{31,28}} | collective-permute-start | bytes 18874376 | tf_op jit(solution)/shard_map/ppermute | solution.py:26
  590.8 15.6 %copy-start.3 = (f32[512,1024]{1,0:T(8,128)S(1)}, f32[512,1024]{1,0:T(8,128)}, u32[]{:S(2)}) copy-start(f32[512,1024]{1,0:T(8,128)} %param.8) | copy-start | bytes 6291460
  601.1 349.0 %collective-permute-start.1 = (bf16[4096,768]{1,0:T(8,128)(2,1)}, bf16[4096,768]{1,0:T(8,128)(2,1)}, u32[]{:S(2)}, u32[]{:S(2)}) collective-permute-start(bf16[4096,768]{1,0:T(8,128)(2,1)} %broadcast_select_fusion), channel_id=1, source_target_pairs={{0,2},{1,3},{4,6},{5,7},{9,11},{10,8},{13,15},{14,12},{18,16},{19,... | collective-permute-start | bytes 18874376 | tf_op jit(solution)/shard_map/ppermute | solution.py:26
  950.1 18.2 %copy-start.1 = (bf16[1024,1536]{1,0:T(8,128)(2,1)S(1)}, bf16[1024,1536]{1,0:T(8,128)(2,1)}, u32[]{:S(2)}) copy-start(bf16[1024,1536]{1,0:T(8,128)(2,1)} %param.7) | copy-start | bytes 9437188
Sparse Core Ops, SparseCore 0:
  28.4 209.9 reduce-scatter.2
  240.6 175.4 all-gather.4
  418.2 32.6 all-gather.6
  453.9 44.5 reduce-scatter.4
  500.5 383.0 all-gather.10
  885.1 48.1 all-gather.8

commit v2 on v1

v2 whole, which is shorter than its diff:
```python
import jax
import jax.numpy as jnp
from jax import lax
from jax.sharding import PartitionSpec as P

F32 = jnp.float32
BF16 = jnp.bfloat16


def mm(a, b, ca, cb):
    return lax.dot_general(a, b, (((ca,), (cb,)), ((), ())), preferred_element_type=F32)


def spread(block, owner, n_dp, n_t, later):
    me = lax.axis_index("tensor")
    mine = me ^ owner(lax.axis_index("dp"))
    step = n_t // 2
    while step:
        pairs = []
        for d in range(n_dp):
            for k in range(0, n_t, 2 * step):
                src = owner(d) ^ k
                pairs.append((d * n_t + src, d * n_t + (src ^ step)))
        got = lax.ppermute(block, ("dp", "tensor"), pairs)
        if step == n_t // 2:
            got, later = lax.optimization_barrier((got, later))
        block = jnp.where(mine % (2 * step) == step, got, block)
        step //= 2
    return block, later


def gather_by_permutes(block, axis, n, hop):
    count = n // hop
    me = lax.axis_index(axis)
    group = me // hop
    got = [block]
    for r in range(1, count):
        pairs = [(p, (p // hop + r) % count * hop + p % hop) for p in range(n)]
        got.append(lax.ppermute(block, axis, pairs))
    return got, group, count


def in_order(got, group, count):
    out = jnp.zeros((count,) + got[0].shape, got[0].dtype)
    for r in range(count):
        out = lax.dynamic_update_slice_in_dim(out, got[r][None], lax.rem(group - r + count, count), 0)
    return out


def shards(inputs, out_grads, left_factor, right_factor, left_basis, right_basis):
    n_dp, n_t = lax.axis_size("dp"), lax.axis_size("tensor")
    krows, kcols = left_factor.shape
    mrows, mcols = right_factor.shape
    dp = lax.axis_index("dp")
    right_low = right_basis.astype(BF16)
    left_low = left_basis.astype(BF16)
    zgot, zgroup, zcount = gather_by_permutes(right_low, "dp", n_dp, 2)
    lgot, lgroup, lcount = gather_by_permutes(left_low, "tensor", n_t, 1)
    partial = mm(inputs, out_grads, 0, 0).astype(BF16)
    summed = lax.psum_scatter(partial, "dp", scatter_dimension=0, tiled=True)
    left_rows = in_order(lgot, lgroup, lcount)
    left_cols = lax.all_to_all(
        left_rows.reshape(n_t, krows, kcols // krows, krows).transpose(0, 2, 1, 3).reshape(n_dp, krows, krows),
        "dp", split_axis=0, concat_axis=0, tiled=True,
    ).reshape(n_dp * krows, krows)
    cross = [(p, p ^ 1) for p in range(n_dp)]
    early = len(zgot) // 2
    first = [lax.ppermute(z, "dp", cross) for z in zgot[:early]]
    summed, zgot, first, left_cols = lax.optimization_barrier((summed, zgot, first, left_cols))
    col_panel = lax.all_gather(summed, "dp", axis=0, tiled=True)
    last = [lax.ppermute(z, "dp", cross) for z in zgot[early:]]
    basis_panel = jnp.zeros((n_dp,) + right_low.shape, BF16)
    for r in range(early):
        at = lax.rem(zgroup - r + zcount, zcount) * 2 + lax.rem(dp, 2)
        basis_panel = lax.dynamic_update_slice_in_dim(basis_panel, zgot[r][None], at, 0)
        basis_panel = lax.dynamic_update_slice_in_dim(basis_panel, first[r][None], at ^ 1, 0)
    col_panel, last, basis_panel = lax.optimization_barrier((col_panel, last, basis_panel))
    for r in range(early, zcount):
        at = lax.rem(zgroup - r + zcount, zcount) * 2 + lax.rem(dp, 2)
        basis_panel = lax.dynamic_update_slice_in_dim(basis_panel, zgot[r][None], at, 0)
        basis_panel = lax.dynamic_update_slice_in_dim(basis_panel, last[r - early][None], at ^ 1, 0)
    basis_panel = basis_panel.reshape(n_dp * mrows, mcols)
    turned = mm(left_cols, col_panel, 0, 0).astype(BF16)
    turned, summed = lax.optimization_barrier((turned, summed))
    turned_rows = lax.all_gather(turned, "tensor", axis=1, tiled=True)
    own = lax.dynamic_slice_in_dim(col_panel, lax.rem(dp * mrows, mcols), mrows, 1)
    parts = jnp.einsum(
        "jkc,rc->jrk", col_panel.reshape(n_t, kcols, mcols), summed, preferred_element_type=F32
    ).astype(BF16)
    own, parts = spread(own, lambda d: d * mrows // mcols, n_dp, n_t, parts)
    gram_left = lax.psum_scatter(
        parts.reshape(n_t * krows, kcols), "tensor", scatter_dimension=0, tiled=True
    ).astype(F32)
    left_new = 0.95 * left_factor + 0.05 * gram_left
    right_new = 0.95 * right_factor + 0.05 * mm(own, col_panel, 0, 0)
    rotated = mm(turned_rows, basis_panel, 1, 0)
    return left_new, right_new, rotated


def solution(mesh):
    spec = P("dp", "tensor")
    return jax.shard_map(
        shards,
        mesh=mesh,
        in_specs=(P("dp", None), spec, spec, spec, spec, spec),
        out_specs=(spec, spec, spec),
        check_vma=False,
    )
```

time: 976 us -> 909 us (0.931)
  waiting for transfers between devices: 831 us -> 705 us
  local copies, waits for them, and re-layouts: 19.6 us -> 52.6 us
  starting transfers between devices: 15.3 us -> 31.2 us
    ppermute x0 -> x10, waiting for transfers between devices: none -> 475 us  [the longest x6 372 us: gather_by_permutes(): got.append(lax.ppermute(block, axis, pairs))]
    all_gather x2 -> x0, waiting for transfers between devices: 293 us -> none  [the longest x1 274 us: shards(): lax.all_gather(right_basis.astype(BF16), 'dp', axis=0, tiled=True)]
    reduce_scatter x1, waiting for transfers between devices: 210 us -> 0.01 us  [shards(): summed = lax.psum_scatter(partial, 'dp', scatter_dimension=0, tiled=True)]
    all_to_all x1, waiting for transfers between devices: 102 us -> 0.01 us  [shards(): lax.all_to_all(left_rows.reshape(n_t, krows, kcols // krows, krows).trans...]
    ppermute x2, waiting for transfers between devices: 0.01 us -> 75.7 us  [spread(): got = lax.ppermute(block, ('dp', 'tensor'), pairs)]
    all_gather x1, waiting for transfers between devices: 49.6 us -> 0.01 us  [shards(): turned_rows = lax.all_gather(turned, 'tensor', axis=1, tiled=True)]
    dynamic_update_slice x0 -> x11, local copies, waits for them, and re-layouts: none -> 24.1 us  [the longest x4 8.07 us: shards(): lax.dynamic_update_slice_in_dim(basis_panel, zgot[r][None], at, 0)]
    all_gather x1, waiting for transfers between devices: 176 us -> 153 us  [shards(): col_panel = lax.all_gather(summed, 'dp', axis=0, tiled=True)]
  transfers between devices with their start and end apart: 9 -> 17, of which waited for: 6 -> 9; matrix products, arithmetic and copies ran while one was open for 8% -> 13% of each run, Pallas kernels for 0% -> 0%
where the time goes in v2:
time: 909 us; the launch traced here: 907 us
  waiting for transfers between devices  705 us (78%)
  matrix products  84.9 us (9%)
  local copies, waits for them, and re-layouts  52.6 us (6%)
  starting transfers between devices  31.2 us (3%)
  other arithmetic  20.3 us (2%)
  between operations  13.9 us (2%)
    ppermute x6, waiting for transfers between devices, gather_by_permutes(): got.append(lax.ppermute(block, axis, pairs))  372 us
    all_gather x1, waiting for transfers between devices, shards(): col_panel = lax.all_gather(summed, 'dp', axis=0, tiled=True)  153 us
    ppermute x2, waiting for transfers between devices, shards(): last = [lax.ppermute(z, 'dp', cross) for z in zgot[early:]]  103 us
    ppermute x2, waiting for transfers between devices, spread(): got = lax.ppermute(block, ('dp', 'tensor'), pairs)  75.7 us
    dot_general x4, matrix products, mm(): lax.dot_general(a, b, (((ca,), (cb,)), ((), ())), preferred_element_type=...  66.6 us
    dot_general x1, matrix products, shards(): jnp.einsum('jkc,rc->jrk', col_panel.reshape(n_t, kcols, mcols), summed, p...  18.3 us
  transfers between devices with their start and end apart: 17, of which 9 were waited for; matrix products, arithmetic and copies ran while one was open for 13% of the time, Pallas kernels for 0%

profile of v2, /device:TPU:0, one launch (start us, length us, event | category | flops | bytes accessed | tf_op | source)
XLA Modules:
  0.0 907.4 jit_solution(4041019502134151689)
XLA Ops:
  7.2 1.8 copy-done
  9.1 19.2 %convolution_convert_fusion = bf16[4096,1536]{1,0:T(8,128)(2,1)} fusion(bf16[1024,4096]{1,0:T(8,128)(2,1)} %param.6, bf16[1024,1536]{1,0:T(8,128)(2,1)S(1)} %copy-done), kind=kOutput, calls=%fused_computation | convolution fusion | flops 12891193344 | bytes 24117248 | tf_op jit(solution)/shard_map/dot_general | solution.py:11
  28.3 2.5 broadcast_in_dim.42
  30.8 1.3 bitcast_dynamic-update-slice_fusion.11
  32.5 2.5 collective-permute-start.6
  35.1 1.4 collective-permute-start.7
  36.5 21.0 %collective-permute-done.5 = bf16[512,1024]{1,0:T(8,128)(2,1)} collective-permute-done((bf16[512,1024]{1,0:T(8,128)(2,1)S(1)}, bf16[512,1024]{1,0:T(8,128)(2,1)}, u32[]{:S(2)}, u32[]{:S(2)}) %collective-permute-start.5) | collective-permute-done | bytes 1048608 | tf_op jit(solution)/shard_map/ppermute | solution.py:39
  57.5 2.3 bitcast_dynamic-update-slice_fusion.10
  59.7 1.0 bitcast_dynamic-update-slice_fusion.9
  60.8 19.7 %collective-permute-done.7 = bf16[512,1024]{1,0:T(8,128)(2,1)S(1)} collective-permute-done((bf16[512,1024]{1,0:T(8,128)(2,1)S(1)}, bf16[512,1024]{1,0:T(8,128)(2,1)S(1)}, u32[]{:S(2)}, u32[]{:S(2)}) %collective-permute-start.7) | collective-permute-done | bytes 1048608 | tf_op jit(solution)/shard_map/ppermute | solution.py:39
  80.5 1.0 bitcast_dynamic-update-slice_fusion.8
  81.5 2.5 fusion.6
  84.1 2.3 pad_maximum_fusion
  86.4 5.9 all-to-all-start
  92.3 2.9 convert_element_type.22
  95.2 1.8 collective-permute-start
  97.0 2.4 collective-permute-start.1
  99.3 1.7 collective-permute-start.2
  101.0 1.5 collective-permute-start.3
  102.5 159.2 %collective-permute-done = bf16[768,1536]{1,0:T(8,128)(2,1)S(1)} collective-permute-done((bf16[768,1536]{1,0:T(8,128)(2,1)S(1)}, bf16[768,1536]{1,0:T(8,128)(2,1)S(1)}, u32[]{:S(2)}, u32[]{:S(2)}) %collective-permute-start) | collective-permute-done | bytes 2359328 | tf_op jit(solution)/shard_map/ppermute | solution.py:39
  261.7 1.6 collective-permute-start.4
  263.3 172.1 %collective-permute-done.1 = bf16[768,1536]{1,0:T(8,128)(2,1)S(1)} collective-permute-done((bf16[768,1536]{1,0:T(8,128)(2,1)S(1)}, bf16[768,1536]{1,0:T(8,128)(2,1)S(1)}, u32[]{:S(2)}, u32[]{:S(2)}) %collective-permute-start.1) | collective-permute-done | bytes 2359328 | tf_op jit(solution)/shard_map/ppermute | solution.py:39
  435.4 1.4 copy-done.4
  437.5 1.4 copy-done.7
  439.1 1.4 collective-permute-start.8
  441.2 6.8 broadcast_in_dim.47
  448.0 1.6 bitcast_dynamic-update-slice_fusion.7
  449.5 1.0 copy-done.8
  450.5 1.6 bitcast_dynamic-update-slice_fusion.6
  452.1 1.5 bitcast_dynamic-update-slice_fusion.5
  453.6 3.2 bitcast_dynamic-update-slice_fusion.4
  456.9 36.7 %collective-permute-done.8 = bf16[768,1536]{1,0:T(8,128)(2,1)} collective-permute-done((bf16[768,1536]{1,0:T(8,128)(2,1)}, bf16[768,1536]{1,0:T(8,128)(2,1)}, u32[]{:S(2)}, u32[]{:S(2)}) %collective-permute-start.8) | collective-permute-done | bytes 2359328 | tf_op jit(solution)/shard_map/ppermute | solution.py:71
  493.5 66.6 %collective-permute-done.9 = bf16[768,1536]{1,0:T(8,128)(2,1)} collective-permute-done((bf16[768,1536]{1,0:T(8,128)(2,1)}, bf16[768,1536]{1,0:T(8,128)(2,1)}, u32[]{:S(2)}, u32[]{:S(2)}) %collective-permute-start.9) | collective-permute-done | bytes 2359328 | tf_op jit(solution)/shard_map/ppermute | solution.py:71
  560.1 152.6 %all-gather.3.cloned.1.call-done = bf16[4096,1536]{1,0:T(8,128)(2,1)} async-done(((bf16[512,1536]{1,0:T(8,128)(2,1)}), bf16[4096,1536]{1,0:T(8,128)(2,1)}) %all-gather.3.cloned.1.call-update) | async-done | bytes 12582928 | tf_op jit(solution)/shard_map/all_gather | solution.py:70
  712.7 11.9 %convolution_convert_fusion.1 = bf16[512,1536]{1,0:T(8,128)(2,1)} fusion(bf16[4096,512]{1,0:T(8,128)(2,1)} %bitcast.5, bf16[4096,1536]{1,0:T(8,128)(2,1)} %all-gather.3.cloned.1.call-done), kind=kOutput, calls=%fused_computation.8 | convolution fusion | flops 6443237376 | bytes 18350080 | tf_op jit(solution)/shard_map/dot_general | solution.py:11
  724.9 10.3 %constant_dynamic-slice_fusion = bf16[4096,768]{1,0:T(8,128)(2,1)} fusion(bf16[4096,1536]{1,0:T(8,128)(2,1)} %all-gather.3.cloned.1.call-done, s32[]{:T(128)S(6)} %select_n.81), kind=kLoop, calls=%fused_computation.23 | loop fusion | bytes 12582916 | tf_op jit(solution)/shard_map/dynamic_slice | solution.py:86
  735.2 5.6 collective-permute-start.10
  740.8 18.3 %convert_bitcast_fusion = bf16[4,512,1024]{2,1,0:T(8,128)(2,1)} fusion(bf16[4,1024,1536]{2,1,0:T(8,128)(2,1)} %bitcast.43, bf16[512,1536]{1,0:T(8,128)(2,1)S(1)} %copy-done.10), kind=kOutput, calls=%fused_computation.7 | convolution fusion | flops 6444548096 | bytes 18350080 | tf_op jit(solution)/shard_map/jkc,rc->jrk/dot_general | solution.py:87
  759.1 75.7 %collective-permute-done.10 = bf16[4096,768]{1,0:T(8,128)(2,1)} collective-permute-done((bf16[4096,768]{1,0:T(8,128)(2,1)}, bf16[4096,768]{1,0:T(8,128)(2,1)}, u32[]{:S(2)}, u32[]{:S(2)}) %collective-permute-start.10) | collective-permute-done | bytes 6291488 | tf_op jit(solution)/shard_map/ppermute | solution.py:24
  834.8 10.2 %broadcast_select_fusion = bf16[4096,768]{1,0:T(8,128)(2,1)} fusion(bf16[4096,768]{1,0:T(8,128)(2,1)} %collective-permute-done.10, pred[]{:T(512)S(6)} %eq.10, bf16[4096,1536]{1,0:T(8,128)(2,1)} %all-gather.3.cloned.1.call-done, s32[]{:T(128)S(6)} %select_n.81), kind=kLoop, calls=%fused_computation.3 | loop fusion | flops 3145728 | bytes 18874372 | tf_op jit(solution)/shard_map/jit(_where)/select_n | solution.py:27
  845.0 3.9 collective-permute-start.11
  848.9 3.4 bitcast_dynamic-update-slice_fusion.3
  852.2 3.3 bitcast_dynamic-update-slice_fusion.2
  855.5 1.6 bitcast_dynamic-update-slice_fusion.1
  857.1 3.6 bitcast_dynamic-update-slice_fusion
  860.7 17.3 %fusion.7 = f32[512,1536]{1,0:T(8,128)} fusion(bf16[512,6144]{1,0:T(8,128)(2,1)} %all-gather.5.cloned.1.call-done, bf16[6144,1536]{1,0:T(8,128)(2,1)} %bitcast.18), kind=kOutput, calls=%fused_computation.25 | convolution fusion | flops 9663676416 | bytes 28311552 | tf_op jit(solution)/shard_map/dot_general | solution.py:11
  878.0 18.3 %multiply_add_fusion = f32[768,1536]{1,0:T(8,128)} fusion(f32[768,1536]{1,0:T(8,128)} %param.9, bf16[4096,1536]{1,0:T(8,128)(2,1)} %all-gather.3.cloned.1.call-done, bf16[4096,768]{1,0:T(8,128)(2,1)} %collective-permute-done.11, bf16[4096,768]{1,0:T(8,128)(2,1)} %broadcast_select_fusion, pred[]{:T(512)S(6)} %eq.9), kind=kOutput, calls=%fused_computation.5 | convolution fusion | flops 9670361088 | bytes 34603008 | tf_op jit(solution)/shard_map/dot_general | solution.py:11
  897.2 3.7 multiply_add_fusion.1
  (37 shorter events, 3.1 us)
Async XLA Ops:
  7.2 1.9 copy-start
  7.2 431.8 %reduce-scatter.3.cloned.1.call-start = ((), (), s32[]{:S(2)}) async-start(), calls=%async_computation.3 | async-start | bytes 14155776 | tf_op jit(solution)/shard_map/reduce_scatter | solution.py:60
  28.2 2.6 copy-start.9
  32.1 25.4 %collective-permute-start.5 = (bf16[512,1024]{1,0:T(8,128)(2,1)S(1)}, bf16[512,1024]{1,0:T(8,128)(2,1)}, u32[]{:S(2)}, u32[]{:S(2)}) collective-permute-start(bf16[512,1024]{1,0:T(8,128)(2,1)S(1)} %get-tuple-element.36), channel_id=1, source_target_pairs={{0,1},{1,2},{2,3},{3,0},{4,5},{5,6},{6,7},{7,4},{8,9},{9,10},{10,1... | collective-permute-start | bytes 3145736 | tf_op jit(solution)/shard_map/ppermute | solution.py:39
  32.5 27.2 %collective-permute-start.6 = (bf16[512,1024]{1,0:T(8,128)(2,1)S(1)}, bf16[512,1024]{1,0:T(8,128)(2,1)S(1)}, u32[]{:S(2)}, u32[]{:S(2)}) collective-permute-start(bf16[512,1024]{1,0:T(8,128)(2,1)S(1)} %get-tuple-element.36), channel_id=1, source_target_pairs={{0,2},{1,3},{2,0},{3,1},{4,6},{5,7},{6,4},{7,5},{8,10},{9,11},{10,... | collective-permute-start | bytes 3145736 | tf_op jit(solution)/shard_map/ppermute | solution.py:39
  35.1 45.4 %collective-permute-start.7 = (bf16[512,1024]{1,0:T(8,128)(2,1)S(1)}, bf16[512,1024]{1,0:T(8,128)(2,1)S(1)}, u32[]{:S(2)}, u32[]{:S(2)}) collective-permute-start(bf16[512,1024]{1,0:T(8,128)(2,1)S(1)} %get-tuple-element.36), channel_id=1, source_target_pairs={{0,3},{1,0},{2,1},{3,2},{4,7},{5,4},{6,5},{7,6},{8,11},{9,8},{10,9... | collective-permute-start | bytes 3145736 | tf_op jit(solution)/shard_map/ppermute | solution.py:39
  86.4 352.6 %all-to-all-start = ((bf16[8,512,512]{2,1,0:T(8,128)(2,1)}), bf16[8,512,512]{2,1,0:T(8,128)(2,1)}, u32[]{:S(2)}, u32[]{:S(2)}) async-start(bf16[8,512,512]{2,1,0:T(8,128)(2,1)} %bitcast.42), calls=%async_computation.1 | async-start | bytes 8388608 | tf_op jit(solution)/shard_map/all_to_all | solution.py:62
  92.3 620.5 %all-gather.3.cloned.1.call-start = ((), (), s32[]{:S(2)}) async-start(), calls=%async_computation.4 | async-start | bytes 14155776 | tf_op jit(solution)/shard_map/all_gather | solution.py:70
  95.2 166.5 %collective-permute-start = (bf16[768,1536]{1,0:T(8,128)(2,1)S(1)}, bf16[768,1536]{1,0:T(8,128)(2,1)S(1)}, u32[]{:S(2)}, u32[]{:S(2)}) collective-permute-start(bf16[768,1536]{1,0:T(8,128)(2,1)S(1)} %convert_element_type.22), channel_id=1, source_target_pairs={{0,8},{4,12},{8,16},{12,20},{16,24},{20,28},{24,0},{28,4},{1,9},{5... | collective-permute-start | bytes 7077896 | tf_op jit(solution)/shard_map/ppermute | solution.py:39
  97.0 338.4 %collective-permute-start.1 = (bf16[768,1536]{1,0:T(8,128)(2,1)S(1)}, bf16[768,1536]{1,0:T(8,128)(2,1)S(1)}, u32[]{:S(2)}, u32[]{:S(2)}) collective-permute-start(bf16[768,1536]{1,0:T(8,128)(2,1)S(1)} %convert_element_type.22), channel_id=1, source_target_pairs={{0,16},{4,20},{8,24},{12,28},{16,0},{20,4},{24,8},{28,12},{1,17},{... | collective-permute-start | bytes 7077896 | tf_op jit(solution)/shard_map/ppermute | solution.py:39
  99.3 336.1 %collective-permute-start.2 = (bf16[768,1536]{1,0:T(8,128)(2,1)S(1)}, bf16[768,1536]{1,0:T(8,128)(2,1)S(1)}, u32[]{:S(2)}, u32[]{:S(2)}) collective-permute-start(bf16[768,1536]{1,0:T(8,128)(2,1)S(1)} %convert_element_type.22), channel_id=1, source_target_pairs={{0,24},{4,28},{8,0},{12,4},{16,8},{20,12},{24,16},{28,20},{1,25},{... | collective-permute-start | bytes 7077896 | tf_op jit(solution)/shard_map/ppermute | solution.py:39
  101.0 334.4 %collective-permute-start.3 = (bf16[768,1536]{1,0:T(8,128)(2,1)S(1)}, bf16[768,1536]{1,0:T(8,128)(2,1)S(1)}, u32[]{:S(2)}, u32[]{:S(2)}) collective-permute-start(bf16[768,1536]{1,0:T(8,128)(2,1)S(1)} %convert_element_type.22), channel_id=1, source_target_pairs={{0,4},{4,0},{8,12},{12,8},{16,20},{20,16},{24,28},{28,24},{1,5},{5... | collective-permute-start | bytes 7077896 | tf_op jit(solution)/shard_map/ppermute | solution.py:68
  261.7 173.7 %copy-start.5 = (bf16[768,1536]{1,0:T(8,128)(2,1)}, bf16[768,1536]{1,0:T(8,128)(2,1)S(1)}, u32[]{:S(2)}) copy-start(bf16[768,1536]{1,0:T(8,128)(2,1)S(1)} %collective-permute-done) | copy-start | bytes 7077892
  261.7 177.2 %collective-permute-start.4 = (bf16[768,1536]{1,0:T(8,128)(2,1)S(1)}, bf16[768,1536]{1,0:T(8,128)(2,1)}, u32[]{:S(2)}, u32[]{:S(2)}) collective-permute-start(bf16[768,1536]{1,0:T(8,128)(2,1)S(1)} %collective-permute-done), channel_id=1, source_target_pairs={{0,4},{4,0},{8,12},{12,8},{16,20},{20,16},{24,28},{28,24},{1,5},{5... | collective-permute-start | bytes 7077896 | tf_op jit(solution)/shard_map/ppermute | solution.py:68
  435.4 1.4 copy-start.4
  435.4 2.1 copy-start.2
  437.5 1.4 copy-start.7
  439.0 421.8 %all-gather.5.cloned.1.call-start = ((), (), s32[]{:S(2)}) async-start(), calls=%async_computation.6 | async-start | bytes 7864320 | tf_op jit(solution)/shard_map/all_gather | solution.py:85
  439.1 54.5 %collective-permute-start.8 = (bf16[768,1536]{1,0:T(8,128)(2,1)}, bf16[768,1536]{1,0:T(8,128)(2,1)}, u32[]{:S(2)}, u32[]{:S(2)}) collective-permute-start(bf16[768,1536]{1,0:T(8,128)(2,1)} %copy-done.4), channel_id=1, source_target_pairs={{0,4},{4,0},{8,12},{12,8},{16,20},{20,16},{24,28},{28,24},{1,5},{5... | collective-permute-start | bytes 7077896 | tf_op jit(solution)/shard_map/ppermute | solution.py:71
  440.5 119.6 %collective-permute-start.9 = (bf16[768,1536]{1,0:T(8,128)(2,1)}, bf16[768,1536]{1,0:T(8,128)(2,1)}, u32[]{:S(2)}, u32[]{:S(2)}) collective-permute-start(bf16[768,1536]{1,0:T(8,128)(2,1)} %copy-done.2), channel_id=1, source_target_pairs={{0,4},{4,0},{8,12},{12,8},{16,20},{20,16},{24,28},{28,24},{1,5},{5... | collective-permute-start | bytes 7077896 | tf_op jit(solution)/shard_map/ppermute | solution.py:71
  448.0 2.5 copy-start.8
  448.0 4.1 copy-start.6
  724.6 172.5 %reduce-scatter.5.cloned.1.call-start = ((), (), s32[]{:S(2)}) async-start(), calls=%async_computation.5 | async-start | bytes 5242880 | tf_op jit(solution)/shard_map/reduce_scatter | solution.py:91
  724.9 16.0 %copy-start.10 = (bf16[512,1536]{1,0:T(8,128)(2,1)S(1)}, bf16[512,1536]{1,0:T(8,128)(2,1)}, u32[]{:S(2)}) copy-start(bf16[512,1536]{1,0:T(8,128)(2,1)} %reduce-scatter.3.cloned.1.call-done) | copy-start | bytes 4718596
  735.2 99.6 %collective-permute-start.10 = (bf16[4096,768]{1,0:T(8,128)(2,1)}, bf16[4096,768]{1,0:T(8,128)(2,1)}, u32[]{:S(2)}, u32[]{:S(2)}) collective-permute-start(bf16[4096,768]{1,0:T(8,128)(2,1)} %constant_dynamic-slice_fusion), channel_id=1, source_target_pairs={{0,2},{4,6},{9,11},{13,15},{18,16},{22,20},{27,25},{31,29}} | collective-permute-start | bytes 18874376 | tf_op jit(solution)/shard_map/ppermute | solution.py:24
  845.0 33.1 %collective-permute-start.11 = (bf16[4096,768]{1,0:T(8,128)(2,1)}, bf16[4096,768]{1,0:T(8,128)(2,1)}, u32[]{:S(2)}, u32[]{:S(2)}) collective-permute-start(bf16[4096,768]{1,0:T(8,128)(2,1)} %broadcast_select_fusion), channel_id=1, source_target_pairs={{0,1},{2,3},{4,5},{6,7},{9,8},{11,10},{13,12},{15,14},{18,19},{16,... | collective-permute-start | bytes 18874376 | tf_op jit(solution)/shard_map/ppermute | solution.py:24
  848.9 6.6 copy-start.3
  878.0 22.9 %copy-start.1 = (bf16[1024,1536]{1,0:T(8,128)(2,1)S(1)}, bf16[1024,1536]{1,0:T(8,128)(2,1)}, u32[]{:S(2)}) copy-start(bf16[1024,1536]{1,0:T(8,128)(2,1)} %param.7) | copy-start | bytes 9437188
Sparse Core Ops, SparseCore 0:
  28.4 403.4 reduce-scatter.2
  439.1 273.6 all-gather.2
  724.7 56.5 all-gather.4
  849.0 48.1 reduce-scatter.4
